TPU v7x, 512 devices: a whole 4x8x8 slice. The times are simulated.
512 devices in a mesh: dp: 16 (over x_hi, y), ctx: 32 (over z, x_lo, core).
Axes of the slice: x: 4 (x_hi: 2, x_lo: 2; x = x_hi * 2 + x_lo), y: 8, z: 8, core: 2. Of those that a mesh axis runs over, the one named last changes fastest.
Arguments:
- tokens: bfloat16 [16, 4096, 8192], P('dp', 'ctx')
- qkv_weight: bfloat16 [8192, 384], P('dp')
- out_grad: bfloat16 [16, 4096, 128], P('dp', 'ctx'), may hold values from -0.0625 to 0.0625
Outputs:
- attn_out: bfloat16 [16, 4096, 128], P('dp', 'ctx')
- qkv_grad: bfloat16 [8192, 384], P('dp')
All inputs are finite; a program needn't handle non-finite values.
Results may differ from a plain program's by a relative error of at most 0.03.
Values may be sent and summed in bfloat16 or wider, within the bound.
No kernel may reach another device: no remote copies, remote signals or barrier semaphores. Data moves between devices by JAX's collectives and lax.ppermute only.
A program may use at most 64 MiB of HBM per device.

v0:
```python
import math
import jax
import jax.numpy as jnp
from jax import lax
from jax.sharding import PartitionSpec as P

z_weight = 0.001
masked_fill = -1e30


def stored_positions(first_row, number, half_rows, ctx_count):
    indices = first_row + jnp.arange(number, dtype=jnp.int32)
    device_index = indices // (2 * half_rows)
    inside = indices % (2 * half_rows)
    block_index = jnp.where(inside < half_rows, device_index, 2 * ctx_count - 1 - device_index)
    return block_index * half_rows + inside % half_rows


def contract_last(left, right):
    return lax.dot_general(
        left, right, (((1,), (1,)), ((), ())), preferred_element_type=jnp.float32
    )


def contract_first(left, right):
    return lax.dot_general(
        left, right, (((0,), (0,)), ((), ())), preferred_element_type=jnp.float32
    )


def on_device(tokens, qkv_weight, out_grad):
    ctx_count = lax.axis_size("ctx")
    feature_rows = tokens[0]
    cotangent = out_grad[0]
    row_count = feature_rows.shape[0]
    half_rows = row_count // 2
    width = qkv_weight.shape[1]
    head_size = width // 3
    score_scale = 1.0 / math.sqrt(head_size)
    columns = lax.all_to_all(tokens, "dp", split_axis=2, concat_axis=0, tiled=True)
    flat_columns = columns.reshape(-1, columns.shape[2])
    projected = jnp.dot(
        feature_rows,
        lax.all_gather(qkv_weight, "dp", axis=0, tiled=True),
        preferred_element_type=jnp.float32,
    )
    qkv = projected.astype(jnp.bfloat16)
    queries = qkv[:, :head_size]
    own_pairs = qkv[:, head_size:]
    gathered = lax.all_gather(own_pairs, "ctx", axis=0, tiled=True)
    key_rows = gathered[:, :head_size]
    value_rows = gathered[:, head_size:]
    own_positions = stored_positions(
        lax.axis_index("ctx") * row_count, row_count, half_rows, ctx_count
    )
    all_positions = stored_positions(0, row_count * ctx_count, half_rows, ctx_count)
    allowed = all_positions[None, :] <= own_positions[:, None]
    scores = jnp.where(allowed, contract_last(queries, key_rows) * score_scale, masked_fill)
    row_top = jnp.max(scores, axis=1)
    log_total = row_top + jnp.log(jnp.sum(jnp.exp(scores - row_top[:, None]), axis=1))
    probs = jnp.where(allowed, jnp.exp(scores - log_total[:, None]), 0.0)
    probs_low = probs.astype(jnp.bfloat16)
    attn_rows = jnp.dot(probs_low, value_rows, preferred_element_type=jnp.float32).astype(
        jnp.bfloat16
    )
    row_delta = jnp.sum(cotangent.astype(jnp.float32) * attn_rows.astype(jnp.float32), axis=1)
    dprob = contract_last(cotangent, value_rows)
    dscore = probs * (dprob - row_delta[:, None] + 2.0 * z_weight * log_total[:, None])
    dscore_low = dscore.astype(jnp.bfloat16)
    grad_query = (
        jnp.dot(dscore_low, key_rows, preferred_element_type=jnp.float32) * score_scale
    ).astype(jnp.bfloat16)
    query_all, cotangent_all = (
        lax.all_gather(queries, "ctx", axis=0, tiled=True),
        lax.all_gather(cotangent, "ctx", axis=0, tiled=True),
    )
    total_all, delta_all = (
        lax.all_gather(log_total, "ctx", axis=0, tiled=True),
        lax.all_gather(row_delta, "ctx", axis=0, tiled=True),
    )
    own_keys = own_pairs[:, :head_size]
    own_values = own_pairs[:, head_size:]
    allowed_back = own_positions[None, :] <= all_positions[:, None]
    scores_back = jnp.where(
        allowed_back, contract_last(query_all, own_keys) * score_scale, masked_fill
    )
    probs_back = jnp.where(allowed_back, jnp.exp(scores_back - total_all[:, None]), 0.0)
    dprob_back = contract_last(cotangent_all, own_values)
    dscore_back = probs_back * (
        dprob_back - delta_all[:, None] + 2.0 * z_weight * total_all[:, None]
    )
    grad_key = (contract_first(dscore_back.astype(jnp.bfloat16), query_all) * score_scale).astype(
        jnp.bfloat16
    )
    grad_value = contract_first(probs_back.astype(jnp.bfloat16), cotangent_all).astype(jnp.bfloat16)
    grad_rows = jnp.concatenate([grad_query, grad_key, grad_value], axis=1)
    partial_sum = contract_first(flat_columns, lax.all_gather(grad_rows, "dp", axis=0, tiled=True))
    weight_total = lax.psum(partial_sum.astype(jnp.bfloat16), "ctx")
    return (attn_rows[None], weight_total)


def solution(mesh):
    placed = (P("dp", "ctx", None), P("dp", None), P("dp", "ctx", None))
    return jax.shard_map(
        on_device,
        mesh=mesh,
        in_specs=placed,
        out_specs=(P("dp", "ctx", None), P("dp", None)),
        check_vma=False,
    )
```

profile of v0, /device:TPU:4, one launch (start us, length us, event | category | flops | bytes accessed | tf_op | source)
XLA Modules:
  0.0 672.1 jit_solution(11417274959753456730)
XLA Ops:
  7.2 0.7 all-gather.9.cloned.1.call-update
  8.0 126.6 %all-gather.9.cloned.1.call-done = bf16[8192,384]{1,0:T(8,128)(2,1)} async-done(((bf16[512,384]{1,0:T(8,128)(2,1)}), bf16[8192,384]{1,0:T(8,128)(2,1)}) %all-gather.9.cloned.1.call-update) | async-done | bytes 6291472 | tf_op jit(solution)/shard_map/all_gather | solution.py:44
  134.5 4.7 fusion.19
  139.2 0.6 slice.27
  139.9 0.6 slice.26
  140.6 0.5 all-gather.17.cloned.1.call-update
  141.2 6.8 %copy.21 = bf16[1,128,8192]{1,0,2:T(2,128)(2,1)} copy(bf16[1,128,8192]{2,1,0:T(8,128)(2,1)S(1)} %copy-done) | data formatting | bytes 4194304 | tf_op args[0]
  148.0 0.6 broadcast.369
  148.6 45.2 %reduce = bf16[8192,128]{1,0:T(8,128)(2,1)S(1)} reduce(bf16[8192,1,128]{2,1,0:T(2,128)(2,1)} %bitcast.59, bf16[]{:T(256)} %broadcast.369), dimensions={1}, to_apply=%bitcast.52.reduce_sub_computation | reduce | bytes 4194306
  193.8 2.1 reshape.196
  195.9 7.6 %all-to-all-start = ((bf16[16,2,32768]{2,1,0:T(2,128)(2,1)}), bf16[16,2,32768]{2,1,0:T(2,128)(2,1)S(1)}, u32[]{:S(2)}, u32[]{:S(2)}) async-start(bf16[16,2,32768]{2,1,0:T(2,128)(2,1)} %reshape.196), calls=%async_computation | async-start | bytes 4194304 | tf_op jit(solution)/shard_map/all_to_all | solution.py:40
  203.7 3.5 all-gather.11.cloned.1.call-done
  207.2 1.9 fusion.69
  209.1 0.4 exponential_reduce_fusion
  209.6 0.7 multiply_reduce_fusion
  210.4 32.5 %all-gather.2 = f32[32,1,128]{2,1,0:T(1,128)S(1)} all-gather(f32[1,1,128]{2,1,0:T(1,128)S(1)} %bitcast.68), channel_id=1, replica_groups=mesh['dp'=16,'ctx'=32] {'ctx'}, dimensions={0}, use_global_device_ids=true | all-gather | bytes 16896 | tf_op jit(solution)/shard_map/all_gather | solution.py:79
  242.9 30.6 %all-gather.1 = f32[32,1,128]{2,1,0:T(1,128)S(1)} all-gather(f32[1,1,128]{2,1,0:T(1,128)S(1)} %bitcast.67), channel_id=1, replica_groups=mesh['dp'=16,'ctx'=32] {'ctx'}, dimensions={0}, use_global_device_ids=true | all-gather | bytes 16896 | tf_op jit(solution)/shard_map/all_gather | solution.py:78
  273.5 2.5 all-gather.13.cloned.1.call-done
  276.1 3.3 fusion.6
  279.4 68.4 %all-gather.17.cloned.1.call-done = bf16[1,4096,128]{2,1,0:T(8,128)(2,1)} async-done(((bf16[1,128,128]{2,1,0:T(8,128)(2,1)}), bf16[1,4096,128]{2,1,0:T(8,128)(2,1)}) %all-gather.17.cloned.1.call-update) | async-done | bytes 1048592 | tf_op jit(solution)/shard_map/all_gather | solution.py:75
  347.8 2.4 convolution_convert_fusion.1
  350.3 3.5 fusion.24
  353.8 3.2 fusion.25
  357.0 0.6 pad_maximum_fusion
  357.7 6.7 %reshape.197 = bf16[8192,1,128]{2,1,0:T(2,128)(2,1)} reshape(bf16[16,2,32768]{2,1,0:T(2,128)(2,1)S(1)} %all-to-all-done) | data formatting | bytes 4194304
  364.5 2.5 copy.27
  366.9 2.6 copy.22
  369.6 70.9 %all-gather.15.cloned.1.call-done = bf16[2048,384]{0,1:T(8,128)(2,1)} async-done(((bf16[128,384]{0,1:T(8,128)(2,1)}), bf16[2048,384]{0,1:T(8,128)(2,1)}) %all-gather.15.cloned.1.call-update) | async-done | bytes 1572880 | tf_op jit(solution)/shard_map/all_gather | solution.py:97
  440.5 3.8 fusion.18
  444.3 0.7 copy.23
  445.0 218.4 %all-reduce.2.cloned.1.call-done = bf16[512,384]{0,1:T(8,128)(2,1)} async-done(((bf16[512,384]{0,1:T(8,128)(2,1)}), bf16[512,384]{0,1:T(8,128)(2,1)}) %all-reduce.2.cloned.1.call-update) | async-done | bytes 393232 | tf_op jit(solution)/shard_map/psum | solution.py:98
  663.4 1.9 copy.24
  (26 shorter events, 0.6 us)
Async XLA Ops:
  7.2 127.3 %all-gather.9.cloned.1.call-start = ((), (), s32[]{:S(2)}) async-start(), calls=%async_computation.1 | async-start | bytes 6684672 | tf_op jit(solution)/shard_map/all_gather | solution.py:44
  7.9 133.3 %copy-start = (bf16[1,128,8192]{2,1,0:T(8,128)(2,1)S(1)}, bf16[1,128,8192]{2,1,0:T(8,128)(2,1)}, u32[]{:S(2)}) copy-start(bf16[1,128,8192]{2,1,0:T(8,128)(2,1)} %param.3) | copy-start | bytes 6291460
  7.9 199.3 %all-gather.11.cloned.1.call-start = ((), (), s32[]{:S(2)}) async-start(), calls=%async_computation.2 | async-start | bytes 2162688 | tf_op jit(solution)/shard_map/all_gather | solution.py:50
  139.9 136.2 %all-gather.13.cloned.1.call-start = ((), (), s32[]{:S(2)}) async-start(), calls=%async_computation.3 | async-start | bytes 1081344 | tf_op jit(solution)/shard_map/all_gather | solution.py:74
  140.6 207.2 %all-gather.17.cloned.1.call-start = ((), (), s32[]{:S(2)}) async-start(), calls=%async_computation.6 | async-start | bytes 1081344 | tf_op jit(solution)/shard_map/all_gather | solution.py:75
  195.9 7.6 %copy-start.3 = (bf16[1,128,128]{2,1,0:T(8,128)(2,1)S(1)}, bf16[1,128,128]{2,1,0:T(8,128)(2,1)}, u32[]{:S(2)}) copy-start(bf16[1,128,128]{2,1,0:T(8,128)(2,1)} %param.5) | copy-start | bytes 98308
  195.9 161.8 %all-to-all-start = ((bf16[16,2,32768]{2,1,0:T(2,128)(2,1)}), bf16[16,2,32768]{2,1,0:T(2,128)(2,1)S(1)}, u32[]{:S(2)}, u32[]{:S(2)}) async-start(bf16[16,2,32768]{2,1,0:T(2,128)(2,1)} %reshape.196), calls=%async_computation | async-start | bytes 4194304 | tf_op jit(solution)/shard_map/all_to_all | solution.py:40
  203.5 237.0 %all-gather.15.cloned.1.call-start = ((), (), s32[]{:S(2)}) async-start(), calls=%async_computation.4 | async-start | bytes 1671168 | tf_op jit(solution)/shard_map/all_gather | solution.py:97
  207.2 2.4 copy-start.4
  209.1 1.3 copy-start.2
  347.8 2.4 copy-start.1
  357.6 305.7 %all-reduce.2.cloned.1.call-start = ((), (), s32[]{:S(2)}) async-start(), calls=%async_computation.5 | async-start | bytes 786432 | tf_op jit(solution)/shard_map/psum | solution.py:98
Sparse Core Ops, SparseCore 0:
  11.2 123.2 all-gather.8
  140.0 67.1 all-gather.10
  209.9 66.0 all-gather.12
  278.1 69.7 all-gather.16
  357.8 82.6 all-gather.14
  444.4 218.9 all-reduce.1
where the time goes:
time: 672 us
  waiting for transfers between devices  492 us (73%)
  blocking collectives  63.1 us (9%)
  other arithmetic  46.4 us (7%)
  local copies, waits for them, and re-layouts  25.4 us (4%)
  matrix products  23.5 us (3%)
  between operations  14.2 us (2%)
  starting transfers between devices  7.83 us (1%)
    psum x1, waiting for transfers between devices, on_device(): weight_total = lax.psum(partial_sum.astype(jnp.bfloat16), 'ctx')  218 us
    all_gather x1, waiting for transfers between devices, on_device(): lax.all_gather(qkv_weight, 'dp', axis=0, tiled=True)  127 us
    all_gather x1, waiting for transfers between devices, on_device(): lax.all_gather(grad_rows, 'dp', axis=0, tiled=True)  70.9 us
    all_gather x1, waiting for transfers between devices, on_device(): lax.all_gather(cotangent, 'ctx', axis=0, tiled=True)  68.4 us
    unnamed x1, other arithmetic  45.2 us
    all_gather x1, blocking collectives, on_device(): lax.all_gather(row_delta, 'ctx', axis=0, tiled=True)  32.5 us
    all_gather x1, blocking collectives, on_device(): lax.all_gather(log_total, 'ctx', axis=0, tiled=True)  30.6 us
    unnamed x18, local copies, waits for them, and re-layouts  21.5 us
  transfers between devices with their start and end apart: 7, of which 6 were waited for; matrix products, arithmetic and copies ran while one was open for 13% of the time, Pallas kernels for 0%

commit v1 on v0

--- a/solution.py
+++ b/solution.py
@@ -95,7 +95,7 @@
     grad_value = contract_first(probs_back.astype(jnp.bfloat16), cotangent_all).astype(jnp.bfloat16)
     grad_rows = jnp.concatenate([grad_query, grad_key, grad_value], axis=1)
     partial_sum = contract_first(flat_columns, lax.all_gather(grad_rows, "dp", axis=0, tiled=True))
-    weight_total = lax.psum(partial_sum.astype(jnp.bfloat16), "ctx")
+    weight_total = jnp.sum(lax.all_gather(partial_sum.astype(jnp.bfloat16), "ctx"), axis=0)
     return (attn_rows[None], weight_total)
 
 

time: 672 us -> 559 us (0.83)
  the two profiles are of different devices: /device:TPU:4 before, /device:TPU:1 now
where the time goes in v1:
time: 559 us
  waiting for transfers between devices  359 us (64%)
  blocking collectives  62.8 us (11%)
  other arithmetic  56.6 us (10%)
  local copies, waits for them, and re-layouts  37.2 us (7%)
  matrix products  23.5 us (4%)
  between operations  14.3 us (3%)
    all_gather x1, waiting for transfers between devices, on_device(): lax.all_gather(qkv_weight, 'dp', axis=0, tiled=True)  129 us
    all_gather x1, waiting for transfers between devices, on_device(): lax.all_gather(partial_sum.astype(jnp.bfloat16), 'ctx')  83.3 us
    all_gather x1, waiting for transfers between devices, on_device(): lax.all_gather(grad_rows, 'dp', axis=0, tiled=True)  69.1 us
    all_gather x1, waiting for transfers between devices, on_device(): lax.all_gather(cotangent, 'ctx', axis=0, tiled=True)  68.5 us
    unnamed x1, other arithmetic  45.2 us
    unnamed x19, local copies, waits for them, and re-layouts  33.3 us
    all_gather x1, blocking collectives, on_device(): lax.all_gather(row_delta, 'ctx', axis=0, tiled=True)  32.2 us
    all_gather x1, blocking collectives, on_device(): lax.all_gather(log_total, 'ctx', axis=0, tiled=True)  30.6 us
  transfers between devices with their start and end apart: 7, of which 6 were waited for; matrix products, arithmetic and copies ran while one was open for 15% of the time, Pallas kernels for 0%

profile of v1, /device:TPU:1, one launch (start us, length us, event | category | flops | bytes accessed | tf_op | source)
XLA Modules:
  0.0 558.8 jit_solution(15063627960101908648)
XLA Ops:
  7.2 0.7 all-gather.11.cloned.1.call-update
  8.0 128.5 %all-gather.11.cloned.1.call-done = bf16[8192,384]{1,0:T(8,128)(2,1)} async-done(((bf16[512,384]{1,0:T(8,128)(2,1)}), bf16[8192,384]{1,0:T(8,128)(2,1)}) %all-gather.11.cloned.1.call-update) | async-done | bytes 6291472 | tf_op jit(solution)/shard_map/all_gather | solution.py:44
  136.5 4.7 fusion.19
  141.2 0.6 slice.27
  141.9 0.6 slice.26
  143.2 6.8 %copy.18 = bf16[1,128,8192]{1,0,2:T(2,128)(2,1)} copy(bf16[1,128,8192]{2,1,0:T(8,128)(2,1)S(1)} %copy-done) | data formatting | bytes 4194304 | tf_op args[0]
  150.0 0.6 broadcast.369
  150.6 45.2 %reduce.1 = bf16[8192,128]{1,0:T(8,128)(2,1)S(1)} reduce(bf16[8192,1,128]{2,1,0:T(2,128)(2,1)} %bitcast.64, bf16[]{:T(256)} %broadcast.369), dimensions={1}, to_apply=%bitcast.57.reduce_sub_computation | reduce | bytes 4194306
  195.8 2.1 reshape.197
  197.8 4.8 all-to-all-start
  202.9 5.9 %all-gather.13.cloned.1.call-done = bf16[4096,256]{1,0:T(8,128)(2,1)} async-done(((bf16[128,256]{1,0:T(8,128)(2,1)}), bf16[4096,256]{1,0:T(8,128)(2,1)}) %all-gather.13.cloned.1.call-update) | async-done | bytes 2097168 | tf_op jit(solution)/shard_map/all_gather | solution.py:50
  208.8 1.9 fusion.69
  211.2 0.7 multiply_reduce_fusion
  212.0 32.2 %all-gather.3 = f32[32,1,128]{2,1,0:T(1,128)S(1)} all-gather(f32[1,1,128]{2,1,0:T(1,128)S(1)} %bitcast.74), channel_id=1, replica_groups=mesh['dp'=16,'ctx'=32] {'ctx'}, dimensions={0}, use_global_device_ids=true | all-gather | bytes 16896 | tf_op jit(solution)/shard_map/all_gather | solution.py:79
  244.2 30.6 %all-gather.2 = f32[32,1,128]{2,1,0:T(1,128)S(1)} all-gather(f32[1,1,128]{2,1,0:T(1,128)S(1)} %bitcast.73), channel_id=1, replica_groups=mesh['dp'=16,'ctx'=32] {'ctx'}, dimensions={0}, use_global_device_ids=true | all-gather | bytes 16896 | tf_op jit(solution)/shard_map/all_gather | solution.py:78
  274.8 2.8 all-gather.15.cloned.1.call-done
  277.6 3.3 fusion.6
  280.9 68.5 %all-gather.19.cloned.1.call-done = bf16[1,4096,128]{2,1,0:T(8,128)(2,1)} async-done(((bf16[1,128,128]{2,1,0:T(8,128)(2,1)}), bf16[1,4096,128]{2,1,0:T(8,128)(2,1)}) %all-gather.19.cloned.1.call-update) | async-done | bytes 1048592 | tf_op jit(solution)/shard_map/all_gather | solution.py:75
  349.4 2.4 convolution_convert_fusion.1
  351.8 3.5 fusion.24
  355.4 3.2 fusion.25
  358.5 0.6 pad_maximum_fusion
  359.3 6.7 %reshape.198 = bf16[8192,1,128]{2,1,0:T(2,128)(2,1)} reshape(bf16[16,2,32768]{2,1,0:T(2,128)(2,1)S(1)} %all-to-all-done) | data formatting | bytes 4194304
  366.0 2.5 copy.24
  368.5 2.6 copy.19
  371.1 69.1 %all-gather.17.cloned.1.call-done = bf16[2048,384]{0,1:T(8,128)(2,1)} async-done(((bf16[128,384]{0,1:T(8,128)(2,1)}), bf16[2048,384]{0,1:T(8,128)(2,1)}) %all-gather.17.cloned.1.call-update) | async-done | bytes 1572880 | tf_op jit(solution)/shard_map/all_gather | solution.py:97
  440.2 3.8 fusion.18
  444.0 0.7 copy.20
  444.7 83.3 %all-gather.21.cloned.1.call-done = bf16[16384,384]{0,1:T(8,128)(2,1)} async-done(((bf16[512,384]{0,1:T(8,128)(2,1)}), bf16[16384,384]{0,1:T(8,128)(2,1)}) %all-gather.21.cloned.1.call-update) | async-done | bytes 12582928 | tf_op jit(solution)/shard_map/all_gather | solution.py:98
  528.0 12.8 %copy.25 = bf16[48,8,32,512]{3,2,1,0:T(8,128)(2,1)} copy(bf16[48,8,32,512]{3,1,2,0:T(8,128)(2,1)} %bitcast.66) | data formatting | bytes 25165824
  540.8 10.2 %bitcast_reduce_fusion = bf16[512,384]{0,1:T(8,128)(2,1)S(1)} fusion(bf16[48,8,32,512]{3,2,1,0:T(8,128)(2,1)} %copy.25), kind=kLoop, calls=%fused_computation | loop fusion | flops 6094848 | bytes 12976128 | tf_op jit(solution)/shard_map/reduce_sum | solution.py:98
  551.1 0.9 copy.21
  (28 shorter events, 1.6 us)
Async XLA Ops:
  7.2 129.3 %all-gather.11.cloned.1.call-start = ((), (), s32[]{:S(2)}) async-start(), calls=%async_computation.1 | async-start | bytes 6684672 | tf_op jit(solution)/shard_map/all_gather | solution.py:44
  7.9 135.3 %copy-start = (bf16[1,128,8192]{2,1,0:T(8,128)(2,1)S(1)}, bf16[1,128,8192]{2,1,0:T(8,128)(2,1)}, u32[]{:S(2)}) copy-start(bf16[1,128,8192]{2,1,0:T(8,128)(2,1)} %param.3) | copy-start | bytes 6291460
  7.9 200.9 %all-gather.13.cloned.1.call-start = ((), (), s32[]{:S(2)}) async-start(), calls=%async_computation.2 | async-start | bytes 2162688 | tf_op jit(solution)/shard_map/all_gather | solution.py:50
  141.8 135.8 %all-gather.15.cloned.1.call-start = ((), (), s32[]{:S(2)}) async-start(), calls=%async_computation.3 | async-start | bytes 1081344 | tf_op jit(solution)/shard_map/all_gather | solution.py:74
  142.6 206.8 %all-gather.19.cloned.1.call-start = ((), (), s32[]{:S(2)}) async-start(), calls=%async_computation.5 | async-start | bytes 1081344 | tf_op jit(solution)/shard_map/all_gather | solution.py:75
  197.8 4.9 copy-start.3
  197.8 161.4 %all-to-all-start = ((bf16[16,2,32768]{2,1,0:T(2,128)(2,1)}), bf16[16,2,32768]{2,1,0:T(2,128)(2,1)S(1)}, u32[]{:S(2)}, u32[]{:S(2)}) async-start(bf16[16,2,32768]{2,1,0:T(2,128)(2,1)} %reshape.197), calls=%async_computation | async-start | bytes 4194304 | tf_op jit(solution)/shard_map/all_to_all | solution.py:40
  202.7 237.5 %all-gather.17.cloned.1.call-start = ((), (), s32[]{:S(2)}) async-start(), calls=%async_computation.4 | async-start | bytes 1671168 | tf_op jit(solution)/shard_map/all_gather | solution.py:97
  208.8 2.4 copy-start.4
  210.7 1.3 copy-start.2
  349.4 2.4 copy-start.1
  359.2 168.8 %all-gather.21.cloned.1.call-start = ((), (), s32[]{:S(2)}) async-start(), calls=%async_computation.6 | async-start | bytes 12976128 | tf_op jit(solution)/shard_map/all_gather | solution.py:98
Sparse Core Ops, SparseCore 0:
  11.2 125.2 all-gather.10
  142.0 66.7 all-gather.12
  211.5 66.0 all-gather.14
  279.6 69.7 all-gather.18
  359.3 80.8 all-gather.16
  444.1 83.8 all-gather.20
